TPU v7x, 256 devices: a whole 4x4x8 slice. The times are simulated.
256 devices in a mesh: dp: 8 (over z), label: 32 (over y, x, core).
Axes of the slice: x: 4, y: 4, z: 8, core: 2. Of those that a mesh axis runs over, the one named last changes fastest.
Arguments:
- enc: bfloat16 [262144, 768], P(('dp', 'label')), may hold values from -6 to 6
- proj: bfloat16 [768, 768], replicated, may hold values from -0.21875 to 0.21875
- head_weight: bfloat16 [4096, 768], P('label'), may hold values from -0.21875 to 0.21875
- shortlist: int32 [2048, 4], P(('dp', 'label')), may hold values from 0 to 31, all different within a row; in each aligned block of 8 rows (0 to 7, 8 to 15, ...) at most 2 rows name the same one
- positives: int32 [262144, 8], P(('dp', 'label')), may hold values from 0 to 511
- weight_num: int32 [4096], P('label'), may hold values from 1 to 16
- weight_den: int32 [4096], P('label'), may hold values from 1 to 16
Outputs:
- grad_enc: float32 [262144, 768], P(('dp', 'label'))
- grad_proj: float32 [768, 768], replicated
- grad_head: float32 [4096, 768], P('label', 'dp')
Inputs may be any that keep to these rules, and one draw needn't show every extreme that they name: `shortlist`: each row names 4 different clusters; among the rows of one device no cluster is named by more than 2 rows, and in every draw some cluster is named by exactly 2 rows of some device; every cluster is named somewhere.
All inputs are finite; a program needn't handle non-finite values.
Results may differ from a plain program's by a relative error of at most 0.005.
Values may be sent and summed in bfloat16 or wider, within the bound.
A program may use at most 128 MiB of HBM per device.

v0:
```python
import jax
import jax.numpy as jnp
from jax import lax
from jax.sharding import PartitionSpec as P


def contract(left, right, left_dim, right_dim):
    return lax.dot_general(
        left, right, (((left_dim,), (right_dim,)), ((), ())), preferred_element_type=jnp.float32
    )


def cluster_grads(hidden_rows, cluster_rows, cluster_scale, wanted, keeping):
    cluster_size = cluster_rows.shape[-2]
    sample_block = hidden_rows.shape[1]
    label_iota = jnp.arange(cluster_size, dtype=jnp.int32)
    logits = jnp.einsum(
        "msd,ld->msl", hidden_rows, cluster_rows, preferred_element_type=jnp.float32
    )
    target = jnp.zeros(logits.shape, jnp.bool_)
    for column in range(wanted.shape[2]):
        target = target | (wanted[:, :, column, None] == label_iota)
    scaled = cluster_scale * (jax.nn.sigmoid(logits) - target.astype(jnp.float32)) / sample_block
    grad_logits = (scaled * keeping[:, None, None]).astype(jnp.bfloat16)
    grad_part = jnp.einsum(
        "msl,ld->msd", grad_logits, cluster_rows, preferred_element_type=jnp.float32
    ).astype(jnp.bfloat16)
    grad_cluster = jnp.einsum(
        "msl,msd->ld", grad_logits, hidden_rows, preferred_element_type=jnp.float32
    )
    return (grad_part, grad_cluster)


def shards(enc, proj, head_weight, shortlist, positives, weight_num, weight_den):
    owners = lax.axis_size("label")
    block_count, beam_width = shortlist.shape
    samples, model_width = enc.shape
    sample_block = samples // block_count
    cluster_size = head_weight.shape[0]
    positive_count = positives.shape[1]
    pair_count = block_count * beam_width
    hidden = jnp.dot(enc, proj, preferred_element_type=jnp.float32).astype(jnp.bfloat16)
    hidden_blocks = hidden.reshape(block_count, sample_block, model_width)
    wanted_blocks = positives.reshape(block_count, sample_block, positive_count)
    capacity = max(2, 2 * pair_count // owners)
    slot_count = owners * capacity
    pair_owner = shortlist.reshape(pair_count)
    pair_iota = jnp.arange(pair_count, dtype=jnp.int32)
    earlier = (pair_owner[:, None] == pair_owner[None, :]) & (
        pair_iota[None, :] < pair_iota[:, None]
    )
    pair_rank = jnp.sum(earlier.astype(jnp.int32), axis=1)
    pair_slot = pair_owner * capacity + pair_rank
    slot_iota = jnp.arange(slot_count, dtype=jnp.int32)
    placed = pair_slot[None, :] == slot_iota[:, None]
    occupied = jnp.any(placed, axis=1).astype(jnp.int32)
    source_pair = jnp.sum(jnp.where(placed, pair_iota[None, :], 0), axis=1)
    source_block = source_pair // beam_width
    source_slot = source_pair % beam_width
    send_rows = jnp.take(hidden_blocks, source_block, axis=0)
    send_wanted = (
        jnp.take(wanted_blocks, source_block, axis=0) - (source_slot * cluster_size)[:, None, None]
    )
    recv_rows, recv_wanted, recv_occupied = (
        lax.all_to_all(send_rows, "label", split_axis=0, concat_axis=0, tiled=True),
        lax.all_to_all(send_wanted, "label", split_axis=0, concat_axis=0, tiled=True),
        lax.all_to_all(occupied, "label", split_axis=0, concat_axis=0, tiled=True),
    )
    cluster_scale = weight_num.astype(jnp.float32) / weight_den.astype(jnp.float32)
    grad_part, weight_part = cluster_grads(
        recv_rows, head_weight, cluster_scale, recv_wanted, recv_occupied.astype(jnp.float32)
    )
    returned = lax.all_to_all(grad_part, "label", split_axis=0, concat_axis=0, tiled=True)
    block_pick = jnp.sum(
        placed.reshape(slot_count, block_count, beam_width).astype(jnp.int32), axis=2
    ).T.astype(jnp.bfloat16)
    grad_hidden = jnp.einsum(
        "bm,msd->bsd", block_pick, returned, preferred_element_type=jnp.float32
    )
    grad_hidden = grad_hidden.reshape(samples, model_width).astype(jnp.bfloat16)
    grad_enc = contract(grad_hidden, proj, 1, 1)
    grad_proj = lax.psum(contract(enc, grad_hidden, 0, 0), ("dp", "label"))
    grad_head = lax.psum_scatter(weight_part, "dp", scatter_dimension=1, tiled=True)
    return (grad_enc, grad_proj, grad_head)


def solution(mesh):
    placed = (
        P(("dp", "label"), None),
        P(),
        P("label", None),
        P(("dp", "label"), None),
        P(("dp", "label"), None),
        P("label"),
        P("label"),
    )
    return jax.shard_map(
        shards,
        mesh=mesh,
        in_specs=placed,
        out_specs=(P(("dp", "label"), None), P(), P("label", "dp")),
        check_vma=False,
    )
```

profile of v0, /device:TPU:2, one launch (start us, length us, event | category | flops | bytes accessed | tf_op | source)
XLA Modules:
  0.0 717.9 jit_solution(10684612803308153281)
XLA Ops:
  8.0 0.0 copy-start
  8.0 0.9 copy.28
  8.9 0.1 eq.157
  9.0 0.2 convert_reduce_fusion.1
  9.2 0.1 fusion.15
  9.3 0.7 reshape.137
  10.0 7.6 %all-to-all-start.2 = ((s32[32,2,1]{1,2,0:T(1,128)}), s32[32,2,1]{1,2,0:T(1,128)S(1)}, u32[]{:S(2)}, u32[]{:S(2)}) async-start(s32[32,2,1]{1,2,0:T(1,128)} %bitcast.14), calls=%async_computation.2 | async-start | bytes 32768 | tf_op jit(solution)/shard_map/all_to_all | solution.py:67
  17.6 0.1 select_reduce_fusion
  17.8 1.4 gather_fusion.1
  19.1 0.0 copy-done
  19.1 2.7 convolution_convert_fusion.1
  21.8 0.9 select_subtract_fusion
  22.7 6.8 gather_fusion
  29.6 0.0 all-to-all-done.2
  29.6 7.5 %all-to-all-start.1 = ((s32[64,128,8]{1,2,0:T(8,128)}), s32[64,128,8]{1,2,0:T(8,128)S(1)}, u32[]{:S(2)}, u32[]{:S(2)}) async-start(s32[64,128,8]{1,2,0:T(8,128)} %select_subtract_fusion), calls=%async_computation.1 | async-start | bytes 524288 | tf_op jit(solution)/shard_map/all_to_all | solution.py:66
  37.1 10.9 %broadcast_select_fusion = bf16[64,128,768]{2,1,0:T(8,128)(2,1)} fusion(bf16[64,128,768]{2,1,0:T(8,128)(2,1)} %gather_fusion, pred[64]{0:T(512)(128)(4,1)S(1)} %compare_and_fusion), kind=kLoop, calls=%fused_computation.4 | loop fusion | flops 6291456 | bytes 25165888 | tf_op jit(solution)/shard_map/jit(_take)/select_n | solution.py:60
  48.0 0.0 copy-start.2
  48.0 0.0 copy-start.3
  48.0 0.0 copy-start.1
  48.0 0.0 all-to-all-done.1
  48.0 8.2 %all-to-all-start = ((bf16[64,128,768]{2,1,0:T(8,128)(2,1)}), bf16[64,128,768]{2,1,0:T(8,128)(2,1)}, u32[]{:S(2)}, u32[]{:S(2)}) async-start(bf16[64,128,768]{2,1,0:T(8,128)(2,1)} %broadcast_select_fusion), calls=%async_computation | async-start | bytes 25165824 | tf_op jit(solution)/shard_map/all_to_all | solution.py:65
  56.2 0.0 copy-done.2
  56.2 0.0 copy-done.3
  56.2 0.1 multiply_reduce_fusion
  56.3 0.1 mul.57
  56.4 0.2 fusion.21
  56.6 148.6 %all-to-all-done = bf16[64,128,768]{2,1,0:T(8,128)(2,1)} async-done(((bf16[64,128,768]{2,1,0:T(8,128)(2,1)}), bf16[64,128,768]{2,1,0:T(8,128)(2,1)}, u32[]{:S(2)}, u32[]{:S(2)}) %all-to-all-start) | async-done | bytes 12582944 | tf_op jit(solution)/shard_map/all_to_all | solution.py:65
  205.1 0.0 copy-done.1
  205.2 12.7 %multiply_convert_fusion = bf16[64,128,128]{2,1,0:T(8,128)(2,1)} fusion(bf16[64,128,768]{2,1,0:T(8,128)(2,1)} %all-to-all-done, f32[64]{0:T(128)S(1)} %mul.57, s32[64,128]{1,0:T(8,128)S(1)} %bitcast.50, s32[64,128]{1,0:T(8,128)S(1)} %bitcast.51, s32[64,128]{1,0:T(8,128)S(1)} %bitcast.52, s32[64,128]{1,0:T(8,128)S(1)} %bitcast.53, ...), kind=kOutput, calls=%fused_computation.6 | convolution fusion | flops 1634729984 | bytes 15139584 | tf_op jit(solution)/shard_map/msd,ld->msl/dot_general | solution.py:17
  217.8 6.3 convolution_convert_fusion
  224.2 22.9 %copy.33 = bf16[64,128,768]{2,1,0:T(8,128)(2,1)} copy(bf16[64,128,768]{2,0,1:T(8,128)(2,1)S(1)} %convolution_convert_fusion) | data formatting | bytes 25165824 | tf_op jit(solution)/shard_map/convert_element_type | solution.py:27
  247.1 16.4 %all-to-all-start.3 = ((bf16[64,128,768]{2,1,0:T(8,128)(2,1)}), bf16[64,128,768]{2,1,0:T(8,128)(2,1)}, u32[]{:S(2)}, u32[]{:S(2)}) async-start(bf16[64,128,768]{2,1,0:T(8,128)(2,1)} %copy.33), calls=%async_computation.3 | async-start | bytes 25165824 | tf_op jit(solution)/shard_map/all_to_all | solution.py:73
  263.5 0.2 all-reduce.2.cloned.1.call-start
  263.7 0.1 reduce_sum.32
  263.8 0.1 copy.30
  263.9 0.1 convert_reduce_fusion
  264.0 148.7 %all-to-all-done.3 = bf16[64,128,768]{2,1,0:T(8,128)(2,1)} async-done(((bf16[64,128,768]{2,1,0:T(8,128)(2,1)}), bf16[64,128,768]{2,1,0:T(8,128)(2,1)}, u32[]{:S(2)}, u32[]{:S(2)}) %all-to-all-start.3) | async-done | bytes 12582944 | tf_op jit(solution)/shard_map/all_to_all | solution.py:73
  412.7 18.0 %fusion.10 = bf16[8,128,768]{2,0,1:T(8,128)(2,1)S(1)} fusion(bf16[64,128,768]{2,1,0:T(8,128)(2,1)} %all-to-all-done.3, s32[64,8]{0,1:T(8,128)S(1)} %convert_reduce_fusion), kind=kOutput, calls=%fused_computation.24 | convolution fusion | flops 101450240 | bytes 14157824 | tf_op jit(solution)/shard_map/bm,msd->bsd/dot_general | solution.py:77
  430.7 0.3 copy.35
  431.0 2.8 convolution_bitcast_fusion
  433.8 0.0 all-reduce.2.cloned.1.call-update
  433.9 0.0 reduce-scatter.2.cloned.1.call-start
  433.9 10.9 %convolution_bitcast_fusion.1 = f32[128,768]{0,1:T(8,128)} fusion(bf16[64,128,128]{2,1,0:T(8,128)(2,1)} %multiply_convert_fusion, bf16[64,128,768]{2,1,0:T(8,128)(2,1)} %all-to-all-done), kind=kOutput, calls=%fused_computation.26 | convolution fusion | flops 1610612736 | bytes 15073280 | tf_op jit(solution)/shard_map/msl,msd->ld/dot_general | solution.py:28
  444.9 0.0 reduce-scatter.2.cloned.1.call-update
  444.9 4.4 fusion.22
  449.2 258.0 %all-reduce.2.cloned.1.call-done = f32[768,768]{0,1:T(8,128)} async-done(((f32[768,768]{0,1:T(8,128)}), f32[768,768]{0,1:T(8,128)}) %all-reduce.2.cloned.1.call-update) | async-done | bytes 2359312 | tf_op jit(solution)/shard_map/psum | solution.py:82
  707.2 3.0 copy.37
  710.2 0.0 reduce-scatter.2.cloned.1.call-done
  (8 shorter events, 0.1 us)
Async XLA Ops:
  8.0 11.1 %copy-start = (bf16[1024,768]{1,0:T(8,128)(2,1)S(1)}, bf16[1024,768]{1,0:T(8,128)(2,1)}, u32[]{:S(2)}) copy-start(bf16[1024,768]{1,0:T(8,128)(2,1)} %param.7) | copy-start | bytes 4718596
  10.0 19.6 %all-to-all-start.2 = ((s32[32,2,1]{1,2,0:T(1,128)}), s32[32,2,1]{1,2,0:T(1,128)S(1)}, u32[]{:S(2)}, u32[]{:S(2)}) async-start(s32[32,2,1]{1,2,0:T(1,128)} %bitcast.14), calls=%async_computation.2 | async-start | bytes 32768 | tf_op jit(solution)/shard_map/all_to_all | solution.py:67
  29.6 18.4 %all-to-all-start.1 = ((s32[64,128,8]{1,2,0:T(8,128)}), s32[64,128,8]{1,2,0:T(8,128)S(1)}, u32[]{:S(2)}, u32[]{:S(2)}) async-start(s32[64,128,8]{1,2,0:T(8,128)} %select_subtract_fusion), calls=%async_computation.1 | async-start | bytes 524288 | tf_op jit(solution)/shard_map/all_to_all | solution.py:66
  48.0 8.2 %copy-start.2 = (s32[128]{0:T(128)S(1)}, s32[128]{0:T(128)}, u32[]{:S(2)}) copy-start(s32[128]{0:T(128)} %param.13) | copy-start | bytes 1540
  48.0 8.2 %copy-start.3 = (s32[128]{0:T(128)S(1)}, s32[128]{0:T(128)}, u32[]{:S(2)}) copy-start(s32[128]{0:T(128)} %param.12) | copy-start | bytes 1540
  48.0 157.2 %copy-start.1 = (bf16[128,768]{1,0:T(8,128)(2,1)S(1)}, bf16[128,768]{1,0:T(8,128)(2,1)}, u32[]{:S(2)}) copy-start(bf16[128,768]{1,0:T(8,128)(2,1)} %param.9) | copy-start | bytes 589828
  48.0 157.2 %all-to-all-start = ((bf16[64,128,768]{2,1,0:T(8,128)(2,1)}), bf16[64,128,768]{2,1,0:T(8,128)(2,1)}, u32[]{:S(2)}, u32[]{:S(2)}) async-start(bf16[64,128,768]{2,1,0:T(8,128)(2,1)} %broadcast_select_fusion), calls=%async_computation | async-start | bytes 25165824 | tf_op jit(solution)/shard_map/all_to_all | solution.py:65
  247.1 165.6 %all-to-all-start.3 = ((bf16[64,128,768]{2,1,0:T(8,128)(2,1)}), bf16[64,128,768]{2,1,0:T(8,128)(2,1)}, u32[]{:S(2)}, u32[]{:S(2)}) async-start(bf16[64,128,768]{2,1,0:T(8,128)(2,1)} %copy.33), calls=%async_computation.3 | async-start | bytes 25165824 | tf_op jit(solution)/shard_map/all_to_all | solution.py:73
  263.5 443.7 %all-reduce.2.cloned.1.call-start = ((), (), s32[]{:S(2)}) async-start(), calls=%async_computation.5 | async-start | bytes 4718592 | tf_op jit(solution)/shard_map/psum | solution.py:82
  433.9 276.4 %reduce-scatter.2.cloned.1.call-start = ((), (), s32[]{:S(2)}) async-start(), calls=%async_computation.6 | async-start | bytes 442368 | tf_op jit(solution)/shard_map/reduce_scatter | solution.py:83
Sparse Core Ops, SparseCore 0:
  434.0 273.1 all-reduce.1
Sparse Core Ops, SparseCore 1:
  445.0 46.8 reduce-scatter.1
where the time goes:
time: 722 us; the launch traced here: 718 us
  waiting for transfers between devices  555 us (77%)
  matrix products  57.8 us (8%)
  starting transfers between devices  40 us (6%)
  local copies, waits for them, and re-layouts  36.6 us (5%)
  between operations  15.9 us (2%)
  other arithmetic  12.4 us (2%)
    psum x1, waiting for transfers between devices, shards(): grad_proj = lax.psum(contract(enc, grad_hidden, 0, 0), ('dp', 'label'))  258 us
    all_to_all x1, waiting for transfers between devices, shards(): lax.all_to_all(grad_part, 'label', split_axis=0, concat_axis=0, tiled=True)  149 us
    all_to_all x1, waiting for transfers between devices, shards(): lax.all_to_all(send_rows, 'label', split_axis=0, concat_axis=0, tiled=True)  149 us
    convert_element_type x1, local copies, waits for them, and re-layouts, cluster_grads(): grad_part = jnp.einsum('msl,ld->msd', grad_logits, cluster_rows, preferre...  22.9 us
    dot_general x1, matrix products, shards(): jnp.einsum('bm,msd->bsd', block_pick, returned, preferred_element_type=jn...  18 us
    all_to_all x1, starting transfers between devices, shards(): lax.all_to_all(grad_part, 'label', split_axis=0, concat_axis=0, tiled=True)  16.4 us
  transfers between devices with their start and end apart: 6, of which 3 were waited for; matrix products, arithmetic and copies ran while one was open for 6% of the time, Pallas kernels for 0%

commit v1 on v0

--- a/solution.py
+++ b/solution.py
@@ -79,7 +79,7 @@
     )
     grad_hidden = grad_hidden.reshape(samples, model_width).astype(jnp.bfloat16)
     grad_enc = contract(grad_hidden, proj, 1, 1)
-    grad_proj = lax.psum(contract(enc, grad_hidden, 0, 0), ("dp", "label"))
+    grad_proj = lax.psum(lax.psum(contract(enc, grad_hidden, 0, 0), "label"), "dp")
     grad_head = lax.psum_scatter(weight_part, "dp", scatter_dimension=1, tiled=True)
     return (grad_enc, grad_proj, grad_head)
 

time: 722 us -> 696 us (0.964)
  waiting for transfers between devices: 555 us -> 531 us
    psum x1 -> x2, waiting for transfers between devices: 258 us -> 197 us  [the longest x1 126 us: shards(): lax.psum(contract(enc, grad_hidden, 0, 0), 'label')]
    reduce_scatter x1, waiting for transfers between devices: 0.01 us -> 36.2 us  [shards(): lax.psum_scatter(weight_part, 'dp', scatter_dimension=1, tiled=True)]
  transfers between devices with their start and end apart: 6 -> 7, of which waited for: 3 -> 5; matrix products, arithmetic and copies ran while one was open for 6% -> 6% of each run, Pallas kernels for 0% -> 0%
where the time goes in v1:
time: 696 us; the launch traced here: 692 us
  waiting for transfers between devices  531 us (76%)
  matrix products  57.8 us (8%)
  starting transfers between devices  40.1 us (6%)
  local copies, waits for them, and re-layouts  36.6 us (5%)
  between operations  14.1 us (2%)
  other arithmetic  12.4 us (2%)
    all_to_all x1, waiting for transfers between devices, shards(): lax.all_to_all(grad_part, 'label', split_axis=0, concat_axis=0, tiled=True)  149 us
    all_to_all x1, waiting for transfers between devices, shards(): lax.all_to_all(send_rows, 'label', split_axis=0, concat_axis=0, tiled=True)  149 us
    psum x1, waiting for transfers between devices, shards(): lax.psum(contract(enc, grad_hidden, 0, 0), 'label')  126 us
    psum x1, waiting for transfers between devices, shards(): lax.psum(lax.psum(contract(enc, grad_hidden, 0, 0), 'label'), 'dp')  71 us
    reduce_scatter x1, waiting for transfers between devices, shards(): lax.psum_scatter(weight_part, 'dp', scatter_dimension=1, tiled=True)  36.2 us
    convert_element_type x1, local copies, waits for them, and re-layouts, cluster_grads(): grad_part = jnp.einsum('msl,ld->msd', grad_logits, cluster_rows, preferre...  22.9 us
    dot_general x1, matrix products, shards(): jnp.einsum('bm,msd->bsd', block_pick, returned, preferred_element_type=jn...  18 us
    all_to_all x1, starting transfers between devices, shards(): lax.all_to_all(grad_part, 'label', split_axis=0, concat_axis=0, tiled=True)  16.4 us
  transfers between devices with their start and end apart: 7, of which 5 were waited for; matrix products, arithmetic and copies ran while one was open for 6% of the time, Pallas kernels for 0%

profile of v1, /device:TPU:2, one launch (start us, length us, event | category | flops | bytes accessed | tf_op | source)
XLA Modules:
  0.0 691.8 jit_solution(6839907165694888585)
XLA Ops:
  7.2 0.0 copy-start
  7.2 0.9 copy.28
  8.1 0.1 eq.157
  8.1 0.2 convert_reduce_fusion.1
  8.3 0.1 fusion.15
  8.4 0.7 reshape.137
  9.1 7.6 %all-to-all-start.2 = ((s32[32,2,1]{1,2,0:T(1,128)}), s32[32,2,1]{1,2,0:T(1,128)S(1)}, u32[]{:S(2)}, u32[]{:S(2)}) async-start(s32[32,2,1]{1,2,0:T(1,128)} %bitcast.14), calls=%async_computation.2 | async-start | bytes 32768 | tf_op jit(solution)/shard_map/all_to_all | solution.py:67
  16.8 0.1 select_reduce_fusion
  16.9 1.4 gather_fusion.1
  18.3 0.0 copy-done
  18.3 2.7 convolution_convert_fusion.1
  21.0 0.9 select_subtract_fusion
  21.9 6.8 gather_fusion
  28.7 0.0 all-to-all-done.2
  28.7 7.5 %all-to-all-start.1 = ((s32[64,128,8]{1,2,0:T(8,128)}), s32[64,128,8]{1,2,0:T(8,128)S(1)}, u32[]{:S(2)}, u32[]{:S(2)}) async-start(s32[64,128,8]{1,2,0:T(8,128)} %select_subtract_fusion), calls=%async_computation.1 | async-start | bytes 524288 | tf_op jit(solution)/shard_map/all_to_all | solution.py:66
  36.2 10.9 %broadcast_select_fusion = bf16[64,128,768]{2,1,0:T(8,128)(2,1)} fusion(bf16[64,128,768]{2,1,0:T(8,128)(2,1)} %gather_fusion, pred[64]{0:T(512)(128)(4,1)S(1)} %compare_and_fusion), kind=kLoop, calls=%fused_computation.4 | loop fusion | flops 6291456 | bytes 25165888 | tf_op jit(solution)/shard_map/jit(_take)/select_n | solution.py:60
  47.1 0.0 copy-start.2
  47.1 0.0 copy-start.3
  47.1 0.0 copy-start.1
  47.1 0.0 all-to-all-done.1
  47.1 8.2 %all-to-all-start = ((bf16[64,128,768]{2,1,0:T(8,128)(2,1)}), bf16[64,128,768]{2,1,0:T(8,128)(2,1)}, u32[]{:S(2)}, u32[]{:S(2)}) async-start(bf16[64,128,768]{2,1,0:T(8,128)(2,1)} %broadcast_select_fusion), calls=%async_computation | async-start | bytes 25165824 | tf_op jit(solution)/shard_map/all_to_all | solution.py:65
  55.4 0.0 copy-done.2
  55.4 0.0 copy-done.3
  55.4 0.1 multiply_reduce_fusion
  55.5 0.1 mul.57
  55.6 0.2 fusion.21
  55.8 148.6 %all-to-all-done = bf16[64,128,768]{2,1,0:T(8,128)(2,1)} async-done(((bf16[64,128,768]{2,1,0:T(8,128)(2,1)}), bf16[64,128,768]{2,1,0:T(8,128)(2,1)}, u32[]{:S(2)}, u32[]{:S(2)}) %all-to-all-start) | async-done | bytes 12582944 | tf_op jit(solution)/shard_map/all_to_all | solution.py:65
  204.3 0.0 copy-done.1
  204.3 12.7 %multiply_convert_fusion = bf16[64,128,128]{2,1,0:T(8,128)(2,1)} fusion(bf16[64,128,768]{2,1,0:T(8,128)(2,1)} %all-to-all-done, f32[64]{0:T(128)S(1)} %mul.57, s32[64,128]{1,0:T(8,128)S(1)} %bitcast.50, s32[64,128]{1,0:T(8,128)S(1)} %bitcast.51, s32[64,128]{1,0:T(8,128)S(1)} %bitcast.52, s32[64,128]{1,0:T(8,128)S(1)} %bitcast.53, ...), kind=kOutput, calls=%fused_computation.6 | convolution fusion | flops 1634729984 | bytes 15139584 | tf_op jit(solution)/shard_map/msd,ld->msl/dot_general | solution.py:17
  217.0 6.3 convolution_convert_fusion
  223.3 22.9 %copy.33 = bf16[64,128,768]{2,1,0:T(8,128)(2,1)} copy(bf16[64,128,768]{2,0,1:T(8,128)(2,1)S(1)} %convolution_convert_fusion) | data formatting | bytes 25165824 | tf_op jit(solution)/shard_map/convert_element_type | solution.py:27
  246.2 16.4 %all-to-all-start.3 = ((bf16[64,128,768]{2,1,0:T(8,128)(2,1)}), bf16[64,128,768]{2,1,0:T(8,128)(2,1)}, u32[]{:S(2)}, u32[]{:S(2)}) async-start(bf16[64,128,768]{2,1,0:T(8,128)(2,1)} %copy.33), calls=%async_computation.3 | async-start | bytes 25165824 | tf_op jit(solution)/shard_map/all_to_all | solution.py:73
  262.7 0.2 all-reduce.3.cloned.1.call-start
  262.9 0.1 reduce_sum.32
  263.0 0.1 copy.30
  263.1 0.1 convert_reduce_fusion
  263.1 148.7 %all-to-all-done.3 = bf16[64,128,768]{2,1,0:T(8,128)(2,1)} async-done(((bf16[64,128,768]{2,1,0:T(8,128)(2,1)}), bf16[64,128,768]{2,1,0:T(8,128)(2,1)}, u32[]{:S(2)}, u32[]{:S(2)}) %all-to-all-start.3) | async-done | bytes 12582944 | tf_op jit(solution)/shard_map/all_to_all | solution.py:73
  411.9 18.0 %fusion.10 = bf16[8,128,768]{2,0,1:T(8,128)(2,1)S(1)} fusion(bf16[64,128,768]{2,1,0:T(8,128)(2,1)} %all-to-all-done.3, s32[64,8]{0,1:T(8,128)S(1)} %convert_reduce_fusion), kind=kOutput, calls=%fused_computation.24 | convolution fusion | flops 101450240 | bytes 14157824 | tf_op jit(solution)/shard_map/bm,msd->bsd/dot_general | solution.py:77
  429.9 0.3 copy.35
  430.2 2.8 convolution_bitcast_fusion
  433.0 0.0 all-reduce.3.cloned.1.call-update
  433.0 0.0 all-reduce.5.cloned.1.call-start
  433.1 126.3 %all-reduce.3.cloned.1.call-done = f32[768,768]{0,1:T(8,128)} async-done(((f32[768,768]{0,1:T(8,128)}), f32[768,768]{0,1:T(8,128)}) %all-reduce.3.cloned.1.call-update) | async-done | bytes 2359312 | tf_op jit(solution)/shard_map/psum | solution.py:82
  559.3 0.0 all-reduce.5.cloned.1.call-update
  559.4 0.0 reduce-scatter.2.cloned.1.call-start
  559.4 11.0 %convolution_bitcast_fusion.1 = f32[128,768]{0,1:T(8,128)} fusion(bf16[64,128,128]{2,1,0:T(8,128)(2,1)} %multiply_convert_fusion, bf16[64,128,768]{2,1,0:T(8,128)(2,1)} %all-to-all-done), kind=kOutput, calls=%fused_computation.26 | convolution fusion | flops 1610612736 | bytes 15073280 | tf_op jit(solution)/shard_map/msl,msd->ld/dot_general | solution.py:28
  570.4 0.0 reduce-scatter.2.cloned.1.call-update
  570.4 4.4 fusion.22
  574.7 71.0 %all-reduce.5.cloned.1.call-done = f32[768,768]{0,1:T(8,128)} async-done(((f32[768,768]{0,1:T(8,128)}), f32[768,768]{0,1:T(8,128)}) %all-reduce.5.cloned.1.call-update) | async-done | bytes 2359312 | tf_op jit(solution)/shard_map/psum | solution.py:82
  645.8 3.0 copy.37
  648.8 36.2 %reduce-scatter.2.cloned.1.call-done = f32[128,96]{0,1:T(8,128)} async-done(((f32[128,768]{0,1:T(8,128)}), f32[128,96]{0,1:T(8,128)}) %reduce-scatter.2.cloned.1.call-update) | async-done | bytes 49168 | tf_op jit(solution)/shard_map/reduce_scatter | solution.py:83
  (8 shorter events, 0.1 us)
Async XLA Ops:
  7.2 11.1 %copy-start = (bf16[1024,768]{1,0:T(8,128)(2,1)S(1)}, bf16[1024,768]{1,0:T(8,128)(2,1)}, u32[]{:S(2)}) copy-start(bf16[1024,768]{1,0:T(8,128)(2,1)} %param.7) | copy-start | bytes 4718596
  9.1 19.6 %all-to-all-start.2 = ((s32[32,2,1]{1,2,0:T(1,128)}), s32[32,2,1]{1,2,0:T(1,128)S(1)}, u32[]{:S(2)}, u32[]{:S(2)}) async-start(s32[32,2,1]{1,2,0:T(1,128)} %bitcast.14), calls=%async_computation.2 | async-start | bytes 32768 | tf_op jit(solution)/shard_map/all_to_all | solution.py:67
  28.7 18.4 %all-to-all-start.1 = ((s32[64,128,8]{1,2,0:T(8,128)}), s32[64,128,8]{1,2,0:T(8,128)S(1)}, u32[]{:S(2)}, u32[]{:S(2)}) async-start(s32[64,128,8]{1,2,0:T(8,128)} %select_subtract_fusion), calls=%async_computation.1 | async-start | bytes 524288 | tf_op jit(solution)/shard_map/all_to_all | solution.py:66
  47.1 8.2 %copy-start.2 = (s32[128]{0:T(128)S(1)}, s32[128]{0:T(128)}, u32[]{:S(2)}) copy-start(s32[128]{0:T(128)} %param.13) | copy-start | bytes 1540
  47.1 8.2 %copy-start.3 = (s32[128]{0:T(128)S(1)}, s32[128]{0:T(128)}, u32[]{:S(2)}) copy-start(s32[128]{0:T(128)} %param.12) | copy-start | bytes 1540
  47.1 157.2 %copy-start.1 = (bf16[128,768]{1,0:T(8,128)(2,1)S(1)}, bf16[128,768]{1,0:T(8,128)(2,1)}, u32[]{:S(2)}) copy-start(bf16[128,768]{1,0:T(8,128)(2,1)} %param.9) | copy-start | bytes 589828
  47.1 157.2 %all-to-all-start = ((bf16[64,128,768]{2,1,0:T(8,128)(2,1)}), bf16[64,128,768]{2,1,0:T(8,128)(2,1)}, u32[]{:S(2)}, u32[]{:S(2)}) async-start(bf16[64,128,768]{2,1,0:T(8,128)(2,1)} %broadcast_select_fusion), calls=%async_computation | async-start | bytes 25165824 | tf_op jit(solution)/shard_map/all_to_all | solution.py:65
  246.2 165.6 %all-to-all-start.3 = ((bf16[64,128,768]{2,1,0:T(8,128)(2,1)}), bf16[64,128,768]{2,1,0:T(8,128)(2,1)}, u32[]{:S(2)}, u32[]{:S(2)}) async-start(bf16[64,128,768]{2,1,0:T(8,128)(2,1)} %copy.33), calls=%async_computation.3 | async-start | bytes 25165824 | tf_op jit(solution)/shard_map/all_to_all | solution.py:73
  262.7 296.7 %all-reduce.3.cloned.1.call-start = ((), (), s32[]{:S(2)}) async-start(), calls=%async_computation.5 | async-start | bytes 4718592 | tf_op jit(solution)/shard_map/psum | solution.py:82
  433.0 212.7 %all-reduce.5.cloned.1.call-start = ((), (), s32[]{:S(2)}) async-start(), calls=%async_computation.6 | async-start | bytes 4718592 | tf_op jit(solution)/shard_map/psum | solution.py:82
  559.4 125.7 %reduce-scatter.2.cloned.1.call-start = ((), (), s32[]{:S(2)}) async-start(), calls=%async_computation.7 | async-start | bytes 442368 | tf_op jit(solution)/shard_map/reduce_scatter | solution.py:83
Sparse Core Ops, SparseCore 0:
  433.2 126.1 all-reduce.2
  561.7 83.9 all-reduce.4
  648.9 36.1 reduce-scatter.1
